TPU v7x, 32 devices: a whole 2x2x4 slice. The times are simulated.
32 devices in a mesh: dp: 2 (over y), expert: 16 (over z, x, core).
Axes of the slice: x: 2, y: 2, z: 4, core: 2. Of those that a mesh axis runs over, the one named last changes fastest.
Arguments:
- tokens: bfloat16 [4096, 2048], P(('dp', 'expert')), may hold values from -6 to 6
- grad_out: bfloat16 [4096, 2048], P(('dp', 'expert')), may hold values from -6 to 6
- expert_ids: int32 [4096, 8], P(('dp', 'expert')), may hold values from 0 to 15, all different within a row; in each aligned block of 128 rows (0 to 127, 128 to 255, ...) at most 72 rows name the same one
- route_weight: bfloat16 [4096, 8], P(('dp', 'expert')), may hold values from 0.049804688 to 1
- w_gate: bfloat16 [16, 2048, 384], P('expert', 'dp'), may hold values from -0.125 to 0.125
- w_up: bfloat16 [16, 2048, 384], P('expert', 'dp'), may hold values from -0.125 to 0.125
- w_down: bfloat16 [16, 384, 2048], P('expert', None, 'dp'), may hold values from -0.3125 to 0.3125
Outputs:
- grad_tokens: bfloat16 [4096, 2048], P(('dp', 'expert'))
- grad_route: bfloat16 [4096, 8], P(('dp', 'expert'))
Inputs may be any that keep to these rules, and one draw needn't show every extreme that they name: `expert_ids`: each row names 8 different experts; among the 128 rows of one device no expert is named by more than 72 rows, and in every draw some expert is named by exactly 72 rows of some device.
All inputs are finite; a program needn't handle non-finite values.
Results may differ from a plain program's by a relative error of at most 0.012.
Values may be sent and summed in bfloat16 or wider, within the bound.
A program may use at most 128 MiB of HBM per device.

v0:
```python
import jax
import jax.numpy as jnp
from jax import lax
from jax.sharding import PartitionSpec as P


def expert_rows(x_rows, g_rows, weight_rows, gate_mat, up_mat, down_mat):
    gate_pre = jnp.dot(x_rows, gate_mat, preferred_element_type=jnp.float32)
    up_pre = jnp.dot(x_rows, up_mat, preferred_element_type=jnp.float32)
    sigmoid_gate = jax.nn.sigmoid(gate_pre)
    active = gate_pre * sigmoid_gate
    hidden = active * up_pre
    back_hidden = jnp.dot(g_rows, down_mat.T, preferred_element_type=jnp.float32)
    route_grad = jnp.sum(hidden * back_hidden, axis=1)
    scaled = weight_rows.astype(jnp.float32)[:, None] * back_hidden
    slope = sigmoid_gate * (1.0 + gate_pre * (1.0 - sigmoid_gate))
    d_gate = (scaled * up_pre * slope).astype(jnp.bfloat16)
    d_up = (scaled * active).astype(jnp.bfloat16)
    input_grad = jnp.dot(d_gate, gate_mat.T, preferred_element_type=jnp.float32) + jnp.dot(
        d_up, up_mat.T, preferred_element_type=jnp.float32
    )
    return (input_grad.astype(jnp.bfloat16), route_grad.astype(jnp.bfloat16))


def fetch_rows(tokens, grad_out, flat_weight, assign_of, top_k):
    token_of = assign_of // top_k
    rows_x = jnp.take(tokens, token_of, axis=0, mode="fill", fill_value=0)
    rows_g = jnp.take(grad_out, token_of, axis=0, mode="fill", fill_value=0)
    rows_w = jnp.take(flat_weight, assign_of, axis=0, mode="fill", fill_value=0)
    return (rows_x, rows_g, rows_w)


def per_device(tokens, grad_out, expert_ids, route_weight, w_gate, w_up, w_down):
    tok_rows, width_model = tokens.shape
    top_k = expert_ids.shape[1]
    n_assign = tok_rows * top_k
    n_expert = lax.axis_size("expert")
    capacity = 9 * tok_rows * top_k // (8 * n_expert)
    slots_all = n_expert * capacity
    gate_mat, up_mat, down_mat = (
        lax.all_gather(w_gate[0], "dp", axis=0, tiled=True),
        lax.all_gather(w_up[0], "dp", axis=0, tiled=True),
        lax.all_gather(w_down[0], "dp", axis=1, tiled=True),
    )
    flat_ids = expert_ids.reshape(-1)
    flat_weight = route_weight.reshape(-1)
    onehot = (flat_ids[:, None] == jnp.arange(n_expert, dtype=jnp.int32)[None, :]).astype(jnp.int32)
    earlier = jnp.cumsum(onehot, axis=0) - onehot
    slot_of = jnp.sum(earlier * onehot, axis=1)
    placed = flat_ids * capacity + slot_of
    assign_index = jnp.arange(n_assign, dtype=jnp.int32)
    slot_assign = (
        jnp.full((slots_all,), n_assign, jnp.int32).at[placed].set(assign_index, mode="drop")
    )
    send_x, send_g, send_w = fetch_rows(tokens, grad_out, flat_weight, slot_assign, top_k)
    send_x = send_x.reshape(n_expert, capacity, width_model)
    send_g = send_g.reshape(n_expert, capacity, width_model)
    send_w = send_w.reshape(n_expert, capacity)
    got_x, got_g, got_w = (
        lax.all_to_all(send_x, "expert", split_axis=0, concat_axis=0, tiled=True),
        lax.all_to_all(send_g, "expert", split_axis=0, concat_axis=0, tiled=True),
        lax.all_to_all(send_w, "expert", split_axis=0, concat_axis=0, tiled=True),
    )
    out_grad, out_route = expert_rows(
        got_x.reshape(slots_all, width_model),
        got_g.reshape(slots_all, width_model),
        got_w.reshape(slots_all),
        gate_mat,
        up_mat,
        down_mat,
    )
    out_grad = out_grad.reshape(n_expert, capacity, width_model)
    out_route = out_route.reshape(n_expert, capacity)
    back_grad, back_route = (
        lax.all_to_all(out_grad, "expert", split_axis=0, concat_axis=0, tiled=True),
        lax.all_to_all(out_route, "expert", split_axis=0, concat_axis=0, tiled=True),
    )
    part_flat = back_grad.reshape(slots_all, width_model)[placed]
    route_flat = back_route.reshape(slots_all)[placed]
    part_rows = part_flat.reshape(tok_rows, top_k, width_model)
    grad_tokens = jnp.sum(part_rows.astype(jnp.float32), axis=1).astype(jnp.bfloat16)
    grad_route = route_flat.reshape(tok_rows, top_k)
    return (grad_tokens, grad_route)


def solution(mesh):
    return jax.shard_map(
        per_device,
        mesh=mesh,
        in_specs=(
            P(("dp", "expert"), None),
            P(("dp", "expert"), None),
            P(("dp", "expert"), None),
            P(("dp", "expert"), None),
            P("expert", "dp", None),
            P("expert", "dp", None),
            P("expert", None, "dp"),
        ),
        out_specs=(P(("dp", "expert"), None), P(("dp", "expert"), None)),
        check_vma=False,
    )
```

profile of v0, /device:TPU:11, one launch (start us, length us, event | category | flops | bytes accessed | tf_op | source)
XLA Modules:
  0.0 429.3 jit_solution(9125871058928897859)
XLA Ops:
  7.2 0.7 broadcast_multiply_fusion
  7.9 0.8 copy.19
  8.7 0.1 eq.29
  8.8 0.1 eq.25
  8.9 0.8 copy.23
  9.7 0.1 reshape.140
  9.8 0.1 copy.18
  9.9 0.1 mul.53
  10.0 4.5 %reduce-window.6 = s32[16,8,128]{2,1,0:T(8,128)S(1)} reduce-window(s32[16,8,128]{2,1,0:T(8,128)S(1)} %fusion.18, s32[]{:T(128)} %constant.47.clone.1), window={size=1x1x128 pad=0_0x0_0x127_0}, to_apply=%region_0.0 | reduce-window | flops 2080768 | bytes 131076 | tf_op jit(solution)/shard_map/reduce-window
  14.5 0.1 slice.18
  14.6 0.1 copy.21
  14.8 0.1 copy.22
  14.9 0.1 broadcast_add_fusion
  15.0 4.3 %scatter_custom_fusion = s32[1152]{0:T(1024)S(1)} fusion(s32[1024]{0:T(1024)S(1)} %bitcast.55, s32[1024]{0:T(1024)S(1)} %iota.11, s32[]{:T(128)} %constant.31.clone.1), kind=kCustom, calls=%fused_computation.51 | custom fusion | bytes 4612 | tf_op jit(solution)/shard_map/scatter | solution.py:53
  19.4 7.3 %gather_fusion = bf16[1152]{0:T(1024)(128)(2,1)S(1)} fusion(bf16[1024]{0:T(1024)(128)(2,1)S(1)} %reshape.140, s32[2048]{0:T(1024)S(1)} %pad_clamp_fusion.1), kind=kCustom, calls=%fused_computation.2 | custom fusion | bytes 9216 | tf_op jit(solution)/shard_map/jit(_take)/gather | solution.py:29
  26.7 0.7 select_n.53
  27.4 6.5 %all-to-all-start = ((bf16[16,1,72]{2,1,0:T(2,128)(2,1)}), bf16[16,1,72]{2,1,0:T(2,128)(2,1)S(1)}, u32[]{:S(2)}, u32[]{:S(2)}) async-start(bf16[16,1,72]{2,1,0:T(2,128)(2,1)} %select_n.53), calls=%async_computation | async-start | bytes 16384 | tf_op jit(solution)/shard_map/all_to_all | solution.py:62
  33.9 5.9 %gather_fusion.4 = bf16[1152,2048]{1,0:T(8,128)(2,1)} fusion(bf16[128,2048]{1,0:T(8,128)(2,1)S(1)} %copy-done, s32[2048]{0:T(1024)S(1)} %pad_clamp_fusion), kind=kCustom, calls=%fused_computation.1.clone | custom fusion | bytes 9441792 | tf_op jit(solution)/shard_map/jit(_take)/gather | solution.py:27
  39.8 5.9 %gather_fusion.3 = bf16[1152,2048]{1,0:T(8,128)(2,1)} fusion(bf16[128,2048]{1,0:T(8,128)(2,1)S(1)} %copy-done.1, s32[2048]{0:T(1024)S(1)} %pad_clamp_fusion), kind=kCustom, calls=%fused_computation.clone | custom fusion | bytes 9441792 | tf_op jit(solution)/shard_map/jit(_take)/gather | solution.py:28
  45.8 8.5 %broadcast_select_fusion.1 = (bf16[1152,2048]{1,0:T(8,128)(2,1)}, bf16[1152,2048]{1,0:T(8,128)(2,1)}) fusion(bf16[1152,2048]{1,0:T(8,128)(2,1)} %gather_fusion.3, pred[1152]{0:T(1024)(128)(4,1)S(1)} %get-tuple-element.7, bf16[1152,2048]{1,0:T(8,128)(2,1)} %gather_fusion.4), kind=kLoop, calls=%fused_computation.9 | loop fusion | flops 4718592 | bytes 18875520 | tf_op jit(solution)/shard_map/jit(_take)/select_n | solution.py:28
  54.3 109.6 %all_to_all.27 = bf16[16,72,2048]{2,1,0:T(8,128)(2,1)} all-to-all(bf16[16,72,2048]{2,1,0:T(8,128)(2,1)} %bitcast.48), channel_id=1, replica_groups=mesh['dp'=2,'expert'=16] {'expert'}, dimensions={0} | all-to-all | bytes 9437184 | tf_op jit(solution)/shard_map/all_to_all | solution.py:60
  163.8 5.3 %all-to-all-start.1 = ((bf16[16,72,2048]{2,1,0:T(8,128)(2,1)}), bf16[16,72,2048]{2,1,0:T(8,128)(2,1)}, u32[]{:S(2)}, u32[]{:S(2)}) async-start(bf16[16,72,2048]{2,1,0:T(8,128)(2,1)} %bitcast.47), calls=%async_computation.1 | async-start | bytes 9437184 | tf_op jit(solution)/shard_map/all_to_all | solution.py:61
  169.1 0.0 all-gather.11.cloned.1.call-start
  169.1 0.7 all-gather.11.cloned.1.call-update
  169.8 0.0 all-gather.9.cloned.1.call-start
  169.9 0.7 all-gather.9.cloned.1.call-update
  170.6 0.2 all-gather.7.cloned.1.call-start
  170.8 0.5 all-gather.7.cloned.1.call-update
  171.3 0.1 reshape.150
  171.4 27.7 %all-gather.11.cloned.1.call-done = bf16[1,2048,384]{2,1,0:T(8,128)(2,1)} async-done(((bf16[1,1024,384]{2,1,0:T(8,128)(2,1)}), bf16[1,2048,384]{2,1,0:T(8,128)(2,1)}) %all-gather.11.cloned.1.call-update) | async-done | bytes 1572880 | tf_op jit(solution)/shard_map/all_gather | solution.py:41
  199.1 5.1 %fusion.4 = f32[1152,384]{0,1:T(8,128)S(1)} fusion(bf16[1152,2048]{1,0:T(8,128)(2,1)} %bitcast.50, bf16[1,2048,384]{2,1,0:T(8,128)(2,1)} %all-gather.11.cloned.1.call-done), kind=kOutput, calls=%fused_computation.18 | convolution fusion | flops 1811939328 | bytes 8060928 | tf_op jit(solution)/shard_map/dot_general | solution.py:8
  204.2 23.7 %all-gather.9.cloned.1.call-done = bf16[1,2048,384]{2,1,0:T(8,128)(2,1)} async-done(((bf16[1,1024,384]{2,1,0:T(8,128)(2,1)}), bf16[1,2048,384]{2,1,0:T(8,128)(2,1)}) %all-gather.9.cloned.1.call-update) | async-done | bytes 1572880 | tf_op jit(solution)/shard_map/all_gather | solution.py:42
  227.9 6.3 %fusion.7 = f32[1152,384]{0,1:T(8,128)} fusion(bf16[1152,2048]{1,0:T(8,128)(2,1)} %bitcast.51, bf16[1,2048,384]{2,1,0:T(8,128)(2,1)} %all-gather.9.cloned.1.call-done), kind=kOutput, calls=%fused_computation.21 | convolution fusion | flops 1811939328 | bytes 8060928 | tf_op jit(solution)/shard_map/dot_general | solution.py:9
  234.2 22.5 %all-gather.7.cloned.1.call-done = bf16[1,384,2048]{2,1,0:T(8,128)(2,1)} async-done(((bf16[1,384,1024]{2,1,0:T(8,128)(2,1)}), bf16[1,384,2048]{2,1,0:T(8,128)(2,1)}) %all-gather.7.cloned.1.call-update) | async-done | bytes 1572880 | tf_op jit(solution)/shard_map/all_gather | solution.py:43
  256.7 16.1 %all-to-all-done.1 = bf16[16,72,2048]{2,1,0:T(8,128)(2,1)} async-done(((bf16[16,72,2048]{2,1,0:T(8,128)(2,1)}), bf16[16,72,2048]{2,1,0:T(8,128)(2,1)}, u32[]{:S(2)}, u32[]{:S(2)}) %all-to-all-start.1) | async-done | bytes 4718624 | tf_op jit(solution)/shard_map/all_to_all | solution.py:61
  272.8 6.8 %multiply_reduce_fusion = (bf16[1152]{0:T(1024)(128)(2,1)S(1)}, f32[1152,384]{0,1:T(8,128)}) fusion(f32[1152,384]{0,1:T(8,128)} %fusion.7, f32[1152,384]{0,1:T(8,128)S(1)} %fusion.4, bf16[1152,2048]{1,0:T(8,128)(2,1)} %bitcast.5, bf16[1,384,2048]{2,1,0:T(8,128)(2,1)} %all-gather.7.cloned.1.call-done), kind=kOutput, calls=%fused_computation.11 | convolution fusion | flops 1815034752 | bytes 11602176 | tf_op jit(solution)/shard_map/dot_general | solution.py:13
  279.6 0.7 convert_element_type.52
  280.3 4.8 %all-to-all-start.4 = ((bf16[16,1,72]{2,1,0:T(2,128)(2,1)}), bf16[16,1,72]{2,1,0:T(2,128)(2,1)S(1)}, u32[]{:S(2)}, u32[]{:S(2)}) async-start(bf16[16,1,72]{2,1,0:T(2,128)(2,1)} %convert_element_type.52), calls=%async_computation.4 | async-start | bytes 16384 | tf_op jit(solution)/shard_map/all_to_all | solution.py:76
  285.1 5.6 %fusion.2 = f32[1152,2048]{1,0:T(8,128)S(1)} fusion(bf16[1,2048,384]{2,1,0:T(8,128)(2,1)} %all-gather.11.cloned.1.call-done, f32[1152,384]{0,1:T(8,128)S(1)} %fusion.4, f32[1152,384]{0,1:T(8,128)} %fusion.7, f32[1152,384]{0,1:T(8,128)} %get-tuple-element.12, f32[1152]{0:T(1024)S(1)} %reshape.150), kind=kOutput, calls=%fused_computation.16 | convolution fusion | flops 1816805376 | bytes 16323072 | tf_op jit(solution)/shard_map/dot_general | solution.py:19
  290.8 4.5 %fusion = bf16[1152,2048]{1,0:T(8,128)(2,1)} fusion(f32[1152,2048]{1,0:T(8,128)S(1)} %fusion.2, bf16[1,2048,384]{2,1,0:T(8,128)(2,1)S(1)} %copy-done.3, f32[1152,384]{0,1:T(8,128)S(1)} %copy-done.2, f32[1152]{0:T(1024)S(1)} %reshape.150, f32[1152,384]{0,1:T(8,128)S(1)} %fusion.4), kind=kOutput, calls=%fused_computation.7 | convolution fusion | flops 1819754496 | bytes 19272192 | tf_op jit(solution)/shard_map/dot_general | solution.py:19
  295.3 6.0 %all-to-all-start.3 = ((bf16[16,72,2048]{2,1,0:T(8,128)(2,1)}), bf16[16,72,2048]{2,1,0:T(8,128)(2,1)}, u32[]{:S(2)}, u32[]{:S(2)}) async-start(bf16[16,72,2048]{2,1,0:T(8,128)(2,1)} %bitcast.49), calls=%async_computation.3 | async-start | bytes 9437184 | tf_op jit(solution)/shard_map/all_to_all | solution.py:75
  301.4 0.1 reshape.148
  301.5 6.8 %gather_fusion.2 = bf16[1024]{0:T(1024)(128)(2,1)S(1)} fusion(bf16[1152]{0:T(1024)(128)(2,1)S(1)} %reshape.148, s32[1024]{0:T(1024)S(1)} %broadcast_clamp_fusion), kind=kCustom, calls=%fused_computation.4 | custom fusion | bytes 8192 | tf_op jit(solution)/shard_map/gather | solution.py:79
  308.3 0.1 reshape.149
  308.4 0.7 copy.26
  309.1 96.0 %all-to-all-done.3 = bf16[16,72,2048]{2,1,0:T(8,128)(2,1)} async-done(((bf16[16,72,2048]{2,1,0:T(8,128)(2,1)}), bf16[16,72,2048]{2,1,0:T(8,128)(2,1)}, u32[]{:S(2)}, u32[]{:S(2)}) %all-to-all-start.3) | async-done | bytes 4718624 | tf_op jit(solution)/shard_map/all_to_all | solution.py:75
  405.0 11.8 %gather_fusion.1 = bf16[1024,2048]{1,0:T(8,128)(2,1)} fusion(bf16[1152,2048]{1,0:T(8,128)(2,1)} %bitcast.12, s32[1024]{0:T(1024)S(1)} %broadcast_clamp_fusion), kind=kCustom, calls=%fused_computation.3 | custom fusion | bytes 8392704 | tf_op jit(solution)/shard_map/gather | solution.py:78
  416.9 5.9 %bitcast_reduce_fusion = bf16[128,2048]{1,0:T(8,128)(2,1)} fusion(bf16[1024,2048]{1,0:T(8,128)(2,1)} %gather_fusion.1), kind=kLoop, calls=%fused_computation.10 | loop fusion | flops 1835008 | bytes 4718592 | tf_op jit(solution)/shard_map/reduce_sum | solution.py:81
  (24 shorter events, 0.2 us)
Async XLA Ops:
  7.2 26.7 %copy-start = (bf16[128,2048]{1,0:T(8,128)(2,1)S(1)}, bf16[128,2048]{1,0:T(8,128)(2,1)}, u32[]{:S(2)}) copy-start(bf16[128,2048]{1,0:T(8,128)(2,1)} %param.9) | copy-start | bytes 1572868
  27.4 26.9 %all-to-all-start = ((bf16[16,1,72]{2,1,0:T(2,128)(2,1)}), bf16[16,1,72]{2,1,0:T(2,128)(2,1)S(1)}, u32[]{:S(2)}, u32[]{:S(2)}) async-start(bf16[16,1,72]{2,1,0:T(2,128)(2,1)} %select_n.53), calls=%async_computation | async-start | bytes 16384 | tf_op jit(solution)/shard_map/all_to_all | solution.py:62
  33.9 5.9 %copy-start.1 = (bf16[128,2048]{1,0:T(8,128)(2,1)S(1)}, bf16[128,2048]{1,0:T(8,128)(2,1)}, u32[]{:S(2)}) copy-start(bf16[128,2048]{1,0:T(8,128)(2,1)} %param.10) | copy-start | bytes 1572868
  163.8 109.0 %all-to-all-start.1 = ((bf16[16,72,2048]{2,1,0:T(8,128)(2,1)}), bf16[16,72,2048]{2,1,0:T(8,128)(2,1)}, u32[]{:S(2)}, u32[]{:S(2)}) async-start(bf16[16,72,2048]{2,1,0:T(8,128)(2,1)} %bitcast.47), calls=%async_computation.1 | async-start | bytes 9437184 | tf_op jit(solution)/shard_map/all_to_all | solution.py:61
  169.1 30.0 %all-gather.11.cloned.1.call-start = ((), (), s32[]{:S(2)}) async-start(), calls=%async_computation.7 | async-start | bytes 2359296 | tf_op jit(solution)/shard_map/all_gather | solution.py:41
  169.8 58.1 %all-gather.9.cloned.1.call-start = ((), (), s32[]{:S(2)}) async-start(), calls=%async_computation.6 | async-start | bytes 2359296 | tf_op jit(solution)/shard_map/all_gather | solution.py:42
  170.6 86.1 %all-gather.7.cloned.1.call-start = ((), (), s32[]{:S(2)}) async-start(), calls=%async_computation.5 | async-start | bytes 2359296 | tf_op jit(solution)/shard_map/all_gather | solution.py:43
  280.3 15.0 %all-to-all-start.4 = ((bf16[16,1,72]{2,1,0:T(2,128)(2,1)}), bf16[16,1,72]{2,1,0:T(2,128)(2,1)S(1)}, u32[]{:S(2)}, u32[]{:S(2)}) async-start(bf16[16,1,72]{2,1,0:T(2,128)(2,1)} %convert_element_type.52), calls=%async_computation.4 | async-start | bytes 16384 | tf_op jit(solution)/shard_map/all_to_all | solution.py:76
  285.1 5.6 %copy-start.2 = (f32[1152,384]{0,1:T(8,128)S(1)}, f32[1152,384]{0,1:T(8,128)}, u32[]{:S(2)}) copy-start(f32[1152,384]{0,1:T(8,128)} %get-tuple-element.12) | copy-start | bytes 5308420
  285.1 5.6 %copy-start.3 = (bf16[1,2048,384]{2,1,0:T(8,128)(2,1)S(1)}, bf16[1,2048,384]{2,1,0:T(8,128)(2,1)}, u32[]{:S(2)}) copy-start(bf16[1,2048,384]{2,1,0:T(8,128)(2,1)} %all-gather.9.cloned.1.call-done) | copy-start | bytes 4718596
  295.3 109.7 %all-to-all-start.3 = ((bf16[16,72,2048]{2,1,0:T(8,128)(2,1)}), bf16[16,72,2048]{2,1,0:T(8,128)(2,1)}, u32[]{:S(2)}, u32[]{:S(2)}) async-start(bf16[16,72,2048]{2,1,0:T(8,128)(2,1)} %bitcast.49), calls=%async_computation.3 | async-start | bytes 9437184 | tf_op jit(solution)/shard_map/all_to_all | solution.py:75
Sparse Core Ops, SparseCore 0:
  171.4 27.6 all-gather.10
  200.7 27.1 all-gather.8
  229.4 27.1 all-gather.6
where the time goes:
time: 430 us; the launch traced here: 429 us
  waiting for transfers between devices  188 us (44%)
  blocking collectives  110 us (26%)
  local copies, waits for them, and re-layouts  46.7 us (11%)
  matrix products  28.4 us (7%)
  starting transfers between devices  22.9 us (5%)
  other arithmetic  19.9 us (5%)
  between operations  13.9 us (3%)
    all_to_all x1, blocking collectives, per_device(): lax.all_to_all(send_x, 'expert', split_axis=0, concat_axis=0, tiled=True)  110 us
    all_to_all x1, waiting for transfers between devices, per_device(): lax.all_to_all(out_grad, 'expert', split_axis=0, concat_axis=0, tiled=True)  96 us
    all_gather x1, waiting for transfers between devices, per_device(): lax.all_gather(w_gate[0], 'dp', axis=0, tiled=True)  27.7 us
    all_gather x1, waiting for transfers between devices, per_device(): lax.all_gather(w_up[0], 'dp', axis=0, tiled=True)  23.7 us
    all_gather x1, waiting for transfers between devices, per_device(): lax.all_gather(w_down[0], 'dp', axis=1, tiled=True)  22.5 us
    all_to_all x1, waiting for transfers between devices, per_device(): lax.all_to_all(send_g, 'expert', split_axis=0, concat_axis=0, tiled=True)  16.1 us
    gather x1, local copies, waits for them, and re-layouts, per_device(): part_flat = back_grad.reshape(slots_all, width_model)[placed]  11.8 us
  transfers between devices with their start and end apart: 7, of which 5 were waited for; matrix products, arithmetic and copies ran while one was open for 12% of the time, Pallas kernels for 0%

commit v1 on v0

v1 whole, which is shorter than its diff:
```python
import jax
import jax.numpy as jnp
from jax import lax
from jax.sharding import PartitionSpec as P


def expert_rows(x_rows, g_rows, weight_rows, gate_mat, up_mat, down_mat):
    gate_pre = jnp.dot(x_rows, gate_mat, preferred_element_type=jnp.float32)
    up_pre = jnp.dot(x_rows, up_mat, preferred_element_type=jnp.float32)
    sigmoid_gate = jax.nn.sigmoid(gate_pre)
    active = gate_pre * sigmoid_gate
    hidden = active * up_pre
    back_hidden = jnp.dot(g_rows, down_mat.T, preferred_element_type=jnp.float32)
    route_grad = jnp.sum(hidden * back_hidden, axis=1)
    scaled = weight_rows.astype(jnp.float32)[:, None] * back_hidden
    slope = sigmoid_gate * (1.0 + gate_pre * (1.0 - sigmoid_gate))
    d_gate = (scaled * up_pre * slope).astype(jnp.bfloat16)
    d_up = (scaled * active).astype(jnp.bfloat16)
    input_grad = jnp.dot(d_gate, gate_mat.T, preferred_element_type=jnp.float32) + jnp.dot(
        d_up, up_mat.T, preferred_element_type=jnp.float32
    )
    return (input_grad.astype(jnp.bfloat16), route_grad.astype(jnp.bfloat16))


def per_device(tokens, grad_out, expert_ids, route_weight, w_gate, w_up, w_down):
    tok_rows, width_model = tokens.shape
    n_expert = lax.axis_size("expert")
    gate_mat, up_mat, down_mat = (
        lax.all_gather(w_gate[0], "dp", axis=0, tiled=True),
        lax.all_gather(w_up[0], "dp", axis=0, tiled=True),
        lax.all_gather(w_down[0], "dp", axis=1, tiled=True),
    )
    chosen = expert_ids[:, :, None] == jnp.arange(n_expert, dtype=jnp.int32)[None, None, :]
    dense_w = jnp.sum(
        jnp.where(chosen, route_weight[:, :, None].astype(jnp.float32), 0.0), axis=1
    ).astype(jnp.bfloat16)
    weight_rows = lax.all_to_all(dense_w.T, "expert", split_axis=0, concat_axis=0, tiled=True)
    all_x = lax.all_gather(tokens, "expert", axis=0, tiled=True)
    all_g = lax.all_gather(grad_out, "expert", axis=0, tiled=True)
    out_grad, out_route = expert_rows(all_x, all_g, weight_rows.reshape(-1), gate_mat, up_mat, down_mat)
    grad_tokens = lax.psum_scatter(out_grad, "expert", scatter_dimension=0, tiled=True)
    back_route = lax.all_to_all(
        out_route.reshape(n_expert, tok_rows), "expert", split_axis=0, concat_axis=0, tiled=True
    )
    grad_route = jnp.sum(
        jnp.where(chosen, back_route.T[:, None, :].astype(jnp.float32), 0.0), axis=2
    ).astype(jnp.bfloat16)
    return (grad_tokens, grad_route)


def solution(mesh):
    return jax.shard_map(
        per_device,
        mesh=mesh,
        in_specs=(
            P(("dp", "expert"), None),
            P(("dp", "expert"), None),
            P(("dp", "expert"), None),
            P(("dp", "expert"), None),
            P("expert", "dp", None),
            P("expert", "dp", None),
            P("expert", None, "dp"),
        ),
        out_specs=(P(("dp", "expert"), None), P(("dp", "expert"), None)),
        check_vma=False,
    )
```

time: 430 us -> 416 us (0.967)
  the two profiles are of different devices: /device:TPU:11 before, /device:TPU:0 now
where the time goes in v1:
time: 416 us; the launch traced here: 415 us
  waiting for transfers between devices  333 us (80%)
  matrix products  54.6 us (13%)
  between operations  14.2 us (3%)
  blocking collectives  8.99 us (2%)
    reduce_scatter x1, waiting for transfers between devices, per_device(): lax.psum_scatter(out_grad, 'expert', scatter_dimension=0, tiled=True)  101 us
    all_gather x1, waiting for transfers between devices, per_device(): all_x = lax.all_gather(tokens, 'expert', axis=0, tiled=True)  76.5 us
    all_gather x1, waiting for transfers between devices, per_device(): all_g = lax.all_gather(grad_out, 'expert', axis=0, tiled=True)  76.3 us
    all_gather x1, waiting for transfers between devices, per_device(): lax.all_gather(w_gate[0], 'dp', axis=0, tiled=True)  28.9 us
    all_gather x1, waiting for transfers between devices, per_device(): lax.all_gather(w_up[0], 'dp', axis=0, tiled=True)  21 us
    all_gather x1, waiting for transfers between devices, per_device(): lax.all_gather(w_down[0], 'dp', axis=1, tiled=True)  19.7 us
    dot_general x1, matrix products, expert_rows(): jnp.dot(d_up, up_mat.T, preferred_element_type=jnp.float32)  15.1 us
    dot_general x1, matrix products, expert_rows(): jnp.dot(d_gate, gate_mat.T, preferred_element_type=jnp.float32)  14.2 us
  transfers between devices with their start and end apart: 7, of which 7 were waited for; matrix products, arithmetic and copies ran while one was open for 4% of the time, Pallas kernels for 0%

profile of v1, /device:TPU:0, one launch (start us, length us, event | category | flops | bytes accessed | tf_op | source)
XLA Modules:
  0.0 415.4 jit_solution(4736880149228869505)
XLA Ops:
  7.2 0.0 all-gather.17.cloned.1.call-start
  7.2 0.7 all-gather.17.cloned.1.call-update
  7.9 0.0 all-gather.11.cloned.1.call-start
  7.9 0.7 all-gather.11.cloned.1.call-update
  8.6 0.0 all-gather.15.cloned.1.call-start
  8.7 0.7 all-gather.15.cloned.1.call-update
  9.4 0.0 all-gather.13.cloned.1.call-start
  9.4 0.5 all-gather.13.cloned.1.call-update
  10.0 0.0 all-gather.9.cloned.1.call-start
  10.0 0.5 all-gather.9.cloned.1.call-update
  10.5 28.9 %all-gather.17.cloned.1.call-done = bf16[1,2048,384]{2,1,0:T(8,128)(2,1)} async-done(((bf16[1,1024,384]{2,1,0:T(8,128)(2,1)}), bf16[1,2048,384]{2,1,0:T(8,128)(2,1)}) %all-gather.17.cloned.1.call-update) | async-done | bytes 1572880 | tf_op jit(solution)/shard_map/all_gather | solution.py:29
  39.5 76.5 %all-gather.11.cloned.1.call-done = bf16[2048,2048]{1,0:T(8,128)(2,1)} async-done(((bf16[128,2048]{1,0:T(8,128)(2,1)}), bf16[2048,2048]{1,0:T(8,128)(2,1)}) %all-gather.11.cloned.1.call-update) | async-done | bytes 8388624 | tf_op jit(solution)/shard_map/all_gather | solution.py:38
  115.9 6.4 %fusion.3 = f32[2048,384]{0,1:T(8,128)S(1)} fusion(bf16[2048,2048]{1,0:T(8,128)(2,1)} %all-gather.11.cloned.1.call-done, bf16[1,2048,384]{2,1,0:T(8,128)(2,1)} %all-gather.17.cloned.1.call-done), kind=kOutput, calls=%fused_computation.8 | convolution fusion | flops 3221225472 | bytes 13107200 | tf_op jit(solution)/shard_map/dot_general | solution.py:8
  122.3 21.0 %all-gather.15.cloned.1.call-done = bf16[1,2048,384]{2,1,0:T(8,128)(2,1)} async-done(((bf16[1,1024,384]{2,1,0:T(8,128)(2,1)}), bf16[1,2048,384]{2,1,0:T(8,128)(2,1)}) %all-gather.15.cloned.1.call-update) | async-done | bytes 1572880 | tf_op jit(solution)/shard_map/all_gather | solution.py:30
  143.3 8.9 %fusion.6 = f32[2048,384]{0,1:T(8,128)} fusion(bf16[2048,2048]{1,0:T(8,128)(2,1)} %all-gather.11.cloned.1.call-done, bf16[1,2048,384]{2,1,0:T(8,128)(2,1)} %all-gather.15.cloned.1.call-done), kind=kOutput, calls=%fused_computation.11 | convolution fusion | flops 3221225472 | bytes 13107200 | tf_op jit(solution)/shard_map/dot_general | solution.py:9
  152.2 0.0 copy-start.1
  152.2 0.0 copy-start
  152.2 19.7 %all-gather.13.cloned.1.call-done = bf16[1,384,2048]{2,1,0:T(8,128)(2,1)} async-done(((bf16[1,384,1024]{2,1,0:T(8,128)(2,1)}), bf16[1,384,2048]{2,1,0:T(8,128)(2,1)}) %all-gather.13.cloned.1.call-update) | async-done | bytes 1572880 | tf_op jit(solution)/shard_map/all_gather | solution.py:31
  171.9 76.3 %all-gather.9.cloned.1.call-done = bf16[2048,2048]{1,0:T(8,128)(2,1)} async-done(((bf16[128,2048]{1,0:T(8,128)(2,1)}), bf16[2048,2048]{1,0:T(8,128)(2,1)}) %all-gather.9.cloned.1.call-update) | async-done | bytes 8388624 | tf_op jit(solution)/shard_map/all_gather | solution.py:39
  248.2 10.1 %multiply_reduce_fusion = (bf16[2048]{0:T(1024)(128)(2,1)S(1)}, f32[2048,384]{0,1:T(8,128)}) fusion(f32[2048,384]{0,1:T(8,128)} %fusion.6, f32[2048,384]{0,1:T(8,128)S(1)} %fusion.3, bf16[2048,2048]{1,0:T(8,128)(2,1)} %all-gather.9.cloned.1.call-done, bf16[1,384,2048]{2,1,0:T(8,128)(2,1)} %all-gather.13.cloned.1.call-done), kind=kOutput, calls=%fused_computation.1 | convolution fusion | flops 3226728448 | bytes 19402752 | tf_op jit(solution)/shard_map/dot_general | solution.py:13
  258.3 0.6 copy.27
  258.9 3.5 all-to-all-start.1
  262.4 0.0 reduce-scatter.2.cloned.1.call-start
  262.5 0.0 copy-done.1
  262.5 6.3 %all-to-all-done.1 = bf16[16,1,128]{2,1,0:T(2,128)(2,1)S(1)} async-done(((bf16[16,1,128]{2,1,0:T(2,128)(2,1)}), bf16[16,1,128]{2,1,0:T(2,128)(2,1)S(1)}, u32[]{:S(2)}, u32[]{:S(2)}) %all-to-all-start.1) | async-done | bytes 4128 | tf_op jit(solution)/shard_map/all_to_all | solution.py:42
  268.7 0.0 copy-done
  268.8 0.6 select_reduce_fusion
  269.4 9.0 %all_to_all.15 = bf16[16,1,128]{2,1,0:T(2,128)(2,1)S(1)} all-to-all(bf16[16,1,128]{2,1,0:T(2,128)(2,1)S(1)} %copy.25), channel_id=1, replica_groups=mesh['dp'=2,'expert'=16] {'expert'}, dimensions={0} | all-to-all | bytes 8192 | tf_op jit(solution)/shard_map/all_to_all | solution.py:37
  278.4 14.2 %fusion.1 = f32[2048,2048]{1,0:T(8,128)} fusion(f32[2048,384]{0,1:T(8,128)S(1)} %fusion.3, f32[2048,384]{0,1:T(8,128)} %fusion.6, f32[2048,384]{0,1:T(8,128)} %get-tuple-element.5, bf16[1,2048,384]{2,1,0:T(8,128)(2,1)} %all-gather.17.cloned.1.call-done, f32[2048]{0:T(1024)S(1)} %bitcast_convert_fusion), kind=kOutput, calls=%fused_computation.6 | convolution fusion | flops 3229876224 | bytes 27795456 | tf_op jit(solution)/shard_map/dot_general | solution.py:19
  292.6 15.1 %add_convert_fusion = bf16[2048,2048]{1,0:T(8,128)(2,1)} fusion(f32[2048,2048]{1,0:T(8,128)} %fusion.1, f32[2048,384]{0,1:T(8,128)} %get-tuple-element.5, bf16[1,2048,384]{2,1,0:T(8,128)(2,1)} %all-gather.15.cloned.1.call-done, f32[2048]{0:T(1024)S(1)} %bitcast_convert_fusion, f32[2048,384]{0,1:T(8,128)S(1)} %fusion.3), kind=kOutput, calls=%fused_computation | convolution fusion | flops 3235119104 | bytes 33038336 | tf_op jit(solution)/shard_map/dot_general | solution.py:19
  307.7 0.0 reduce-scatter.2.cloned.1.call-update
  307.7 100.8 %reduce-scatter.2.cloned.1.call-done = bf16[128,2048]{1,0:T(8,128)(2,1)} async-done(((bf16[2048,2048]{1,0:T(8,128)(2,1)}), bf16[128,2048]{1,0:T(8,128)(2,1)}) %reduce-scatter.2.cloned.1.call-update) | async-done | bytes 524304 | tf_op jit(solution)/shard_map/reduce_scatter | solution.py:41
  (4 shorter events, 0.0 us)
Async XLA Ops:
  7.2 32.3 %all-gather.17.cloned.1.call-start = ((), (), s32[]{:S(2)}) async-start(), calls=%async_computation.8 | async-start | bytes 2359296 | tf_op jit(solution)/shard_map/all_gather | solution.py:29
  7.9 108.0 %all-gather.11.cloned.1.call-start = ((), (), s32[]{:S(2)}) async-start(), calls=%async_computation.4 | async-start | bytes 8912896 | tf_op jit(solution)/shard_map/all_gather | solution.py:38
  8.6 134.6 %all-gather.15.cloned.1.call-start = ((), (), s32[]{:S(2)}) async-start(), calls=%async_computation.7 | async-start | bytes 2359296 | tf_op jit(solution)/shard_map/all_gather | solution.py:30
  9.4 162.5 %all-gather.13.cloned.1.call-start = ((), (), s32[]{:S(2)}) async-start(), calls=%async_computation.6 | async-start | bytes 2359296 | tf_op jit(solution)/shard_map/all_gather | solution.py:31
  10.0 238.3 %all-gather.9.cloned.1.call-start = ((), (), s32[]{:S(2)}) async-start(), calls=%async_computation.3 | async-start | bytes 8912896 | tf_op jit(solution)/shard_map/all_gather | solution.py:39
  152.2 110.3 %copy-start.1 = (bf16[128,8]{0,1:T(8,128)(2,1)S(1)}, bf16[128,8]{0,1:T(8,128)(2,1)}, u32[]{:S(2)}) copy-start(bf16[128,8]{0,1:T(8,128)(2,1)} %param.10) | copy-start | bytes 6148
  152.2 116.5 %copy-start = (s32[128,8]{0,1:T(8,128)S(1)}, s32[128,8]{0,1:T(8,128)}, u32[]{:S(2)}) copy-start(s32[128,8]{0,1:T(8,128)} %param.9) | copy-start | bytes 12292
  258.9 9.8 %all-to-all-start.1 = ((bf16[16,1,128]{2,1,0:T(2,128)(2,1)}), bf16[16,1,128]{2,1,0:T(2,128)(2,1)S(1)}, u32[]{:S(2)}, u32[]{:S(2)}) async-start(bf16[16,1,128]{2,1,0:T(2,128)(2,1)} %copy.27), calls=%async_computation.2 | async-start | bytes 16384 | tf_op jit(solution)/shard_map/all_to_all | solution.py:42
  262.4 146.1 %reduce-scatter.2.cloned.1.call-start = ((), (), s32[]{:S(2)}) async-start(), calls=%async_computation.5 | async-start | bytes 8912896 | tf_op jit(solution)/shard_map/reduce_scatter | solution.py:41
Sparse Core Ops, SparseCore 0:
  9.5 29.8 all-gather.16
  41.6 74.2 all-gather.10
  117.5 25.7 all-gather.14
  144.7 27.1 all-gather.12
  173.9 74.2 all-gather.8
  307.8 100.6 reduce-scatter.1

commit v2 on v0

--- a/solution.py
+++ b/solution.py
@@ -1,6 +1,10 @@
+import functools
+
 import jax
 import jax.numpy as jnp
 from jax import lax
+from jax.experimental import pallas as pl
+from jax.experimental.pallas import tpu as pltpu
 from jax.sharding import PartitionSpec as P
 
 
@@ -30,7 +34,7 @@
     return (rows_x, rows_g, rows_w)
 
 
-def per_device(tokens, grad_out, expert_ids, route_weight, w_gate, w_up, w_down):
+def per_device_exchange(tokens, grad_out, expert_ids, route_weight, w_gate, w_up, w_down):
     tok_rows, width_model = tokens.shape
     top_k = expert_ids.shape[1]
     n_assign = tok_rows * top_k
@@ -81,6 +85,424 @@
     grad_tokens = jnp.sum(part_rows.astype(jnp.float32), axis=1).astype(jnp.bfloat16)
     grad_route = route_flat.reshape(tok_rows, top_k)
     return (grad_tokens, grad_route)
+
+
+LANES = 128
+MESH = pl.DeviceIdType.MESH
+
+
+def gather_kernel(
+    n_rows, x_in, g_in, route_in, gate_in, up_in, down_in, out_ref, out_route,
+    all_x, all_g, w_in, w_down, part, from_sib, from_row, from_below, from_above,
+    pre, back, d_both,
+    load_sem, weight_load, weight_send, weight_recv,
+    recv, send_up, send_down, send_row, send_sib, send_extra,
+    sib_send, sib_recv, row_send, row_recv, col_send, below_recv, above_recv,
+):
+    me = lax.axis_index("expert")
+    y = lax.axis_index("dp")
+    z, x, core = me // 4, (me // 2) % 2, me % 2
+    top = n_rows - 1
+    tok, width = x_in.shape
+    hidden = gate_in.shape[1]
+    shard = gate_in.shape[0]
+    half = tok // 2
+
+    sib = {"expert": me + 1 - 2 * core}
+    across = {"expert": me + 2 - 4 * x}
+    above = {"expert": me + 4}
+    below = {"expert": me - 4}
+    twin = {"dp": 1 - y}
+
+    upper = z // 2
+    near = z + upper * (top - 2 * z)
+
+    def row_of(k):
+        r = near if k == 0 else (1 - near if k == 1 else k)
+        return r + upper * (top - 2 * r)
+
+    def row_of_traced(k):
+        early = 1 - jnp.minimum(k // 2, 1)
+        r = early * (near + k * (1 - 2 * near)) + (1 - early) * k
+        return r + upper * (top - 2 * r)
+
+    def index(row, col, c):
+        return (row * 2 + col) * 2 + c
+
+    bufs = (all_x, all_g)
+
+    def remote(src, dst, s, r, who):
+        return pltpu.make_async_remote_copy(
+            src_ref=src, dst_ref=dst, send_sem=s, recv_sem=r, device_id=who, device_id_type=MESH
+        )
+
+    def block(p, e, s, who):
+        return remote(bufs[p].at[e], bufs[p].at[e], s, recv.at[p, e], who)
+
+    def wait_block(p, e):
+        pltpu.make_async_copy(bufs[p].at[e], bufs[p].at[e], recv.at[p, e]).wait()
+
+    loads = [
+        pltpu.make_async_copy(x_in, all_x.at[me], load_sem.at[0]),
+        pltpu.make_async_copy(g_in, all_g.at[me, :, pl.ds(0, width)], load_sem.at[1]),
+        pltpu.make_async_copy(route_in, all_g.at[me, :, pl.ds(width, LANES)], load_sem.at[2]),
+    ]
+    rows = pl.ds(pl.multiple_of(y * shard, shard), shard)
+    homes = [
+        w_in.at[rows, pl.ds(0, hidden)],
+        w_in.at[rows, pl.ds(hidden, hidden)],
+        w_down.at[:, rows],
+    ]
+    for cp in loads:
+        cp.start()
+    weight_loads = [
+        pltpu.make_async_copy(src, dst, weight_load.at[i])
+        for i, (src, dst) in enumerate(zip((gate_in, up_in, down_in), homes))
+    ]
+    for cp in weight_loads:
+        cp.start()
+
+    barrier = pltpu.get_barrier_semaphore()
+    for who in (sib, across, twin):
+        pl.semaphore_signal(barrier, inc=1, device_id=who, device_id_type=MESH)
+
+    @pl.when(z > 0)
+    def _():
+        pl.semaphore_signal(barrier, inc=1, device_id=below, device_id_type=MESH)
+
+    @pl.when(z < top)
+    def _():
+        pl.semaphore_signal(barrier, inc=1, device_id=above, device_id_type=MESH)
+
+    pl.semaphore_wait(barrier, 3 + jnp.minimum(z, 1) + jnp.minimum(top - z, 1))
+
+    for cp in loads:
+        cp.wait()
+
+    def up_copy(p, row):
+        return block(p, index(row, x, core), send_up.at[p, row], above)
+
+    def down_copy(p, row):
+        return block(p, index(row, x, core), send_down.at[p, row], below)
+
+    def row_copy(p, row):
+        return block(p, index(row, x, core), send_row.at[p, row], across)
+
+    def sib_copy(p, row, col):
+        return block(p, index(row, col, core), send_sib.at[p, row * 2 + col], sib)
+
+    def extra_copy(way, who):
+        return block(1, index(z, 1 - x, core), send_extra.at[way], who)
+
+    def by_row(p, k):
+        return None if p == 0 or k == 0 or k == 3 else (near == k - 1)
+
+    def row_forward(p, k, action):
+        cond = by_row(p, k)
+        if cond is None:
+            action()
+        else:
+            pl.when(jnp.logical_not(cond))(action)
+
+    for p in (0, 1):
+
+        @pl.when(z < top)
+        def _(p=p):
+            up_copy(p, z).start()
+
+        @pl.when(z > 0)
+        def _(p=p):
+            down_copy(p, z).start()
+
+        row_copy(p, z).start()
+        sib_copy(p, z, x).start()
+
+    weight_copies = []
+    for i, cp in enumerate(weight_loads):
+        cp.wait()
+        c = remote(homes[i], homes[i], weight_send.at[i], weight_recv.at[i], twin)
+        c.start()
+        weight_copies.append(c)
+
+    def column_arrival(p, k):
+        row = row_of(k)
+        wait_block(p, index(row, x, core))
+
+        @pl.when(jnp.logical_and(row < z, z < top))
+        def _():
+            up_copy(p, row).start()
+
+        @pl.when(jnp.logical_and(row > z, z > 0))
+        def _():
+            down_copy(p, row).start()
+
+        row_forward(p, k, lambda: row_copy(p, row).start())
+        sib_copy(p, row, x).start()
+
+    def row_arrival(p, k):
+        row = row_of(k)
+        wait_block(p, index(row, 1 - x, core))
+        if p == 1 and k == 0:
+
+            @pl.when(jnp.logical_and(z > 0, z < top))
+            def _():
+                extra_copy(0, below).start()
+                extra_copy(1, above).start()
+
+        sib_copy(p, row, 1 - x).start()
+
+    for k in (1, 2):
+        for p in (0, 1):
+            column_arrival(p, k)
+            row_arrival(p, k - 1)
+
+    @pl.when(near == 1)
+    def _():
+        column_arrival(0, 3)
+        column_arrival(1, 3)
+
+    for c in weight_copies:
+        c.wait_recv()
+
+    lane = lax.broadcasted_iota(jnp.int32, (half, LANES), 1)
+
+    def chip_of(i):
+        side = i % 2
+        return row_of_traced(i // 2) * 2 + x + side * (1 - 2 * x)
+
+    def compute(i):
+        q = chip_of(i)
+        other = 2 * q + 1 - core
+        wait_block(0, other)
+        wait_block(1, other)
+        pair = pl.ds(2 * q, 2)
+
+        @pl.loop(0, 2 * hidden // 256)
+        def _(j):
+            cols = pl.ds(pl.multiple_of(j * 256, 256), 256)
+            pre[:, cols] = jnp.dot(
+                all_x[pair].reshape(2 * tok, width), w_in[:, cols], preferred_element_type=jnp.float32
+            )
+
+        back[...] = lax.dot_general(
+            all_g[pair, :, pl.ds(0, width)].reshape(2 * tok, width), w_down[...],
+            (((1,), (1,)), ((), ())), preferred_element_type=jnp.float32,
+        )
+
+        @pl.loop(0, 4)
+        def _(r):
+            rs = pl.ds(pl.multiple_of(r * half, half), half)
+            e, off = 2 * q + r // 2, pl.ds(pl.multiple_of((r % 2) * half, half), half)
+            gate_pre = pre[rs, pl.ds(0, hidden)]
+            up_pre = pre[rs, pl.ds(hidden, hidden)]
+            back_hidden = back[rs, :]
+            sig = jax.nn.sigmoid(gate_pre)
+            active = gate_pre * sig
+            route_grad = jnp.sum(active * up_pre * back_hidden, axis=1, keepdims=True)
+            weights = all_g[e, off, pl.ds(width, LANES)].astype(jnp.float32)
+            weight = jnp.sum(jnp.where(lane == me, weights, 0.0), axis=1, keepdims=True)
+            scaled = weight * back_hidden
+            slope = sig * (1.0 + gate_pre * (1.0 - sig))
+            d_both[rs, pl.ds(0, hidden)] = (scaled * up_pre * slope).astype(jnp.bfloat16)
+            d_both[rs, pl.ds(hidden, hidden)] = (scaled * active).astype(jnp.bfloat16)
+            part[e, off, pl.ds(width, LANES)] = jnp.where(lane == me, route_grad, 0.0).astype(jnp.bfloat16)
+
+        @pl.loop(0, width // 256)
+        def _(j):
+            cols = pl.ds(pl.multiple_of(j * 256, 256), 256)
+            res = lax.dot_general(
+                d_both[...], w_in[cols, :], (((1,), (1,)), ((), ())), preferred_element_type=jnp.float32
+            )
+            part[pair, :, cols] = res.astype(jnp.bfloat16).reshape(2, tok, 256)
+
+        to_sib(q).start()
+
+    def to_sib(q):
+        return remote(part.at[2 * q + 1 - core], from_sib.at[q], sib_send.at[q], sib_recv.at[q], sib)
+
+    def add_into(dst, src):
+        dst[...] = (dst[...].astype(jnp.float32) + src[...].astype(jnp.float32)).astype(jnp.bfloat16)
+
+    def finish(i):
+        q = chip_of(i)
+        to_sib(q).wait_recv()
+        add_into(part.at[2 * q + core], from_sib.at[q])
+
+    @pl.loop(0, 2 * n_rows)
+    def _(i):
+        @pl.when(i == 4)
+        def _():
+            for p in (0, 1):
+
+                @pl.when(near == 0)
+                def _(p=p):
+                    column_arrival(p, 3)
+
+                row_arrival(p, 2)
+
+        @pl.when(i == 2 * n_rows - 1)
+        def _():
+            row_arrival(0, 3)
+            row_arrival(1, 3)
+
+        compute(i)
+
+        @pl.when(i > 0)
+        def _():
+            finish(i - 1)
+
+    finish(2 * n_rows - 1)
+
+    def halves(h):
+        return pl.ds(pl.multiple_of(h * half, half), half)
+
+    def row_sum(row, h):
+        return remote(
+            part.at[index(row, 1 - x, core), halves(h)], from_row.at[row, halves(h)],
+            row_send.at[row, h], row_recv.at[row, h], across,
+        )
+
+    def col_up(row, h):
+        return remote(
+            part.at[index(row, x, core), halves(h)], from_below.at[row, halves(h)],
+            col_send.at[row, h], below_recv.at[row, h], above,
+        )
+
+    def col_down(row, h):
+        return remote(
+            part.at[index(row, x, core), halves(h)], from_above.at[row, halves(h)],
+            col_send.at[row, h], above_recv.at[row, h], below,
+        )
+
+    @pl.loop(0, 2 * n_rows)
+    def _(i):
+        row_sum(row_of_traced(top - i // 2), i % 2).start()
+
+    @pl.loop(0, 2 * n_rows)
+    def _(i):
+        row, h = row_of_traced(top - i // 2), i % 2
+        mine = part.at[index(row, x, core), halves(h)]
+        row_sum(row, h).wait_recv()
+        add_into(mine, from_row.at[row, halves(h)])
+
+        @pl.when(jnp.logical_and(row >= z, z > 0))
+        def _():
+            col_up(row, h).wait_recv()
+            add_into(mine, from_below.at[row, halves(h)])
+
+        @pl.when(jnp.logical_and(row <= z, z < top))
+        def _():
+            col_down(row, h).wait_recv()
+            add_into(mine, from_above.at[row, halves(h)])
+
+        @pl.when(row > z)
+        def _():
+            col_up(row, h).start()
+
+        @pl.when(row < z)
+        def _():
+            col_down(row, h).start()
+
+    out_ref[...] = part[me, :, pl.ds(0, width)]
+    out_route[...] = part[me, :, pl.ds(width, LANES)]
+
+    for c in weight_copies:
+        c.wait_send()
+    for k in range(n_rows):
+        row = row_of(k)
+        for p in (0, 1):
+            if k == 0:
+
+                @pl.when(z < top)
+                def _(p=p):
+                    up_copy(p, z).wait_send()
+
+                @pl.when(z > 0)
+                def _(p=p):
+                    down_copy(p, z).wait_send()
+            else:
+
+                @pl.when(jnp.logical_and(row < z, z < top))
+                def _(p=p, row=row):
+                    up_copy(p, row).wait_send()
+
+                @pl.when(jnp.logical_and(row > z, z > 0))
+                def _(p=p, row=row):
+                    down_copy(p, row).wait_send()
+
+            row_forward(p, k, lambda p=p, row=row: row_copy(p, row).wait_send())
+            sib_copy(p, row, x).wait_send()
+            sib_copy(p, row, 1 - x).wait_send()
+
+    @pl.when(jnp.logical_and(z > 0, z < top))
+    def _():
+        extra_copy(0, below).wait_send()
+        extra_copy(1, above).wait_send()
+
+    @pl.loop(0, 2 * n_rows)
+    def _(i):
+        to_sib(i).wait_send()
+        row, h = i // 2, i % 2
+        row_sum(row, h).wait_send()
+
+        @pl.when(row != z)
+        def _():
+            col_up(row, h).wait_send()
+
+
+def per_device_gather(tokens, grad_out, expert_ids, route_weight, w_gate, w_up, w_down):
+    tok, width = tokens.shape
+    n_expert = lax.axis_size("expert")
+    n_rows = n_expert // 4
+    hidden = w_gate.shape[2]
+    chosen = expert_ids[:, :, None] == jnp.arange(LANES, dtype=jnp.int32)[None, None, :]
+    dense = jnp.sum(jnp.where(chosen, route_weight[:, :, None].astype(jnp.float32), 0.0), axis=1)
+    wide = width + LANES
+    bf16, dma = jnp.bfloat16, pltpu.SemaphoreType.DMA
+    vmem = pltpu.VMEM
+    out, routes = pl.pallas_call(
+        functools.partial(gather_kernel, n_rows),
+        out_shape=(
+            jax.ShapeDtypeStruct((tok, width), bf16),
+            jax.ShapeDtypeStruct((tok, LANES), bf16),
+        ),
+        in_specs=[pl.BlockSpec(memory_space=pl.ANY)] * 6,
+        out_specs=(pl.BlockSpec(memory_space=pltpu.VMEM), pl.BlockSpec(memory_space=pltpu.VMEM)),
+        scratch_shapes=[
+            vmem((n_expert, tok, width), bf16),
+            vmem((n_expert, tok, wide), bf16),
+            vmem((width, 2 * hidden), bf16),
+            vmem((hidden, width), bf16),
+            vmem((n_expert, tok, wide), bf16),
+            vmem((n_expert // 2, tok, wide), bf16),
+            vmem((n_rows, tok, wide), bf16),
+            vmem((n_rows, tok, wide), bf16),
+            vmem((n_rows, tok, wide), bf16),
+            vmem((2 * tok, 2 * hidden), jnp.float32),
+            vmem((2 * tok, hidden), jnp.float32),
+            vmem((2 * tok, 2 * hidden), bf16),
+            dma((3,)), dma((3,)), dma((3,)), dma((3,)),
+            dma((2, n_expert)), dma((2, n_rows)), dma((2, n_rows)), dma((2, n_rows)),
+            dma((2, n_expert // 2)), dma((2,)),
+            dma((n_expert // 2,)), dma((n_expert // 2,)),
+            dma((n_rows, 2)), dma((n_rows, 2)), dma((n_rows, 2)), dma((n_rows, 2)), dma((n_rows, 2)),
+        ],
+        compiler_params=pltpu.CompilerParams(
+            collective_id=0, has_side_effects=True, vmem_limit_bytes=60 * 1024 * 1024
+        ),
+    )(tokens, grad_out, dense.astype(bf16), w_gate[0], w_up[0], w_down[0])
+    grad_route = jnp.sum(
+        jnp.where(chosen, routes[:, None, :].astype(jnp.float32), 0.0), axis=2
+    ).astype(bf16)
+    return (out, grad_route)
+
+
+def per_device(*args):
+    n_expert, top_k = lax.axis_size("expert"), args[2].shape[1]
+    grid_fits = lax.axis_size("dp") == 2 and n_expert // 4 == 4 and n_expert % 4 == 0
+    if grid_fits and 2 * top_k >= n_expert:
+        return per_device_gather(*args)
+    return per_device_exchange(*args)
 
 
 def solution(mesh):

time: 430 us -> 176 us (0.41)
  the two profiles are of different devices: /device:TPU:11 before, /device:TPU:0 now
where the time goes in v2:
time: 176 us; the launch traced here: 175 us
  Pallas kernels  169 us (96%)
  local copies, waits for them, and re-layouts  3.45 us (2%)
  other arithmetic  2.13 us (1%)
    pallas_call x1, Pallas kernels, per_device_gather(): pl.pallas_call(functools.partial(gather_kernel, n_rows), out_shape=(jax.S...  169 us

profile of v2, /device:TPU:0, one launch (start us, length us, event | category | flops | bytes accessed | tf_op | source)
XLA Modules:
  0.0 175.4 jit_solution(15493318478003479757)
XLA Ops:
  0.6 0.0 copy-start
  0.6 0.8 copy.11
  1.4 0.0 copy-done
  1.4 0.1 copy.12
  1.5 1.0 select_reduce_fusion.1.route_in
  2.5 169.2 %shard_map.86 = (bf16[128,2048]{1,0:T(8,128)(2,1)}, bf16[128,128]{1,0:T(8,128)(2,1)}) custom-call(bf16[128,2048]{1,0:T(8,128)(2,1)} %x_in.1, bf16[128,2048]{1,0:T(8,128)(2,1)} %g_in.1, bf16[128,128]{1,0:T(8,128)(2,1)} %select_reduce_fusion.1.route_in, bf16[1024,384]{1,0:T(8,128)(2,1)} %bitcast.3, bf16[1024,384]{1,0:T(8,128)(2,1)} %bitcast.4, ...), custom_call_target="tpu_custom_call" | custom-call | tf_op jit(solution)/shard_map/pallas_call | solution.py:463
  171.8 0.8 convert_element_type.16
  172.5 0.4 select_reduce_fusion
  172.9 0.7 copy.13
  173.6 1.9 %copy.15 = bf16[128,2048]{1,0:T(8,128)(2,1)} copy(bf16[128,2048]{1,0:T(8,128)(2,1)} %get-tuple-element.10) | data formatting | bytes 1048576
Async XLA Ops:
  0.6 0.8 copy-start

commit v3 on v2

--- a/solution.py
+++ b/solution.py
@@ -242,24 +242,29 @@
     def row_arrival(p, k):
         row = row_of(k)
         wait_block(p, index(row, 1 - x, core))
-        if p == 1 and k == 0:
-
-            @pl.when(jnp.logical_and(z > 0, z < top))
-            def _():
-                extra_copy(0, below).start()
-                extra_copy(1, above).start()
-
         sib_copy(p, row, 1 - x).start()
 
-    for k in (1, 2):
-        for p in (0, 1):
-            column_arrival(p, k)
-            row_arrival(p, k - 1)
+    @pl.when(near == 0)
+    def _():
+        for k in (1, 2):
+            column_arrival(0, k)
+            row_arrival(0, k - 1)
+            column_arrival(1, k)
+            if k == 1:
+                row_arrival(1, 0)
 
     @pl.when(near == 1)
     def _():
+        for p in (0, 1):
+            column_arrival(p, 1)
+            column_arrival(p, 2)
+            row_arrival(p, 0)
         column_arrival(0, 3)
+        row_arrival(0, 1)
         column_arrival(1, 3)
+        extra_copy(0, below).start()
+        extra_copy(1, above).start()
+        row_arrival(1, 1)
 
     for c in weight_copies:
         c.wait_recv()
@@ -267,8 +272,13 @@
     lane = lax.broadcasted_iota(jnp.int32, (half, LANES), 1)
 
     def chip_of(i):
-        side = i % 2
-        return row_of_traced(i // 2) * 2 + x + side * (1 - 2 * x)
+        last = i // (2 * n_rows - 1)
+        outer = i + jnp.minimum(i // 3, 1) - 5 * last
+        at_five, at_six = jnp.minimum(i // 5, 1), jnp.minimum(i // 6, 1)
+        inner = i + at_five - 2 * at_six + last
+        turn = outer + near * (inner - outer)
+        side = turn % 2
+        return row_of_traced(turn // 2) * 2 + x + side * (1 - 2 * x)
 
     def compute(i):
         q = chip_of(i)
@@ -328,31 +338,6 @@
         to_sib(q).wait_recv()
         add_into(part.at[2 * q + core], from_sib.at[q])
 
-    @pl.loop(0, 2 * n_rows)
-    def _(i):
-        @pl.when(i == 4)
-        def _():
-            for p in (0, 1):
-
-                @pl.when(near == 0)
-                def _(p=p):
-                    column_arrival(p, 3)
-
-                row_arrival(p, 2)
-
-        @pl.when(i == 2 * n_rows - 1)
-        def _():
-            row_arrival(0, 3)
-            row_arrival(1, 3)
-
-        compute(i)
-
-        @pl.when(i > 0)
-        def _():
-            finish(i - 1)
-
-    finish(2 * n_rows - 1)
-
     def halves(h):
         return pl.ds(pl.multiple_of(h * half, half), half)
 
@@ -374,9 +359,50 @@
             col_send.at[row, h], above_recv.at[row, h], below,
         )
 
+    def send_row_sums(step):
+        k = top - step + (near * (2 * step - 1) if step < 2 else 0)
+        row = row_of_traced(k)
+        for h in (0, 1):
+            row_sum(row, h).start()
+
     @pl.loop(0, 2 * n_rows)
     def _(i):
-        row_sum(row_of_traced(top - i // 2), i % 2).start()
+        @pl.when(jnp.logical_and(i == 1, near == 0))
+        def _():
+            column_arrival(0, 3)
+
+        @pl.when(jnp.logical_and(i == 3, near == 0))
+        def _():
+            column_arrival(1, 3)
+
+        @pl.when(i == 4)
+        def _():
+            row_arrival(0, 2)
+            row_arrival(1, 2)
+
+        @pl.when(i == 6 + near)
+        def _():
+            row_arrival(0, 3)
+            row_arrival(1, 3)
+
+        @pl.when(i == 2 * n_rows - 1)
+        def _():
+            finish(i - 1)
+            send_row_sums(0)
+
+            @pl.when(near == 0)
+            def _():
+                row_arrival(1, 1)
+
+        compute(i)
+
+        @pl.when(jnp.logical_and(i > 0, i < 2 * n_rows - 1))
+        def _():
+            finish(i - 1)
+
+    finish(2 * n_rows - 1)
+    for step in range(1, n_rows):
+        send_row_sums(step)
 
     @pl.loop(0, 2 * n_rows)
     def _(i):

time: 176 us -> 162 us (0.920)
  Pallas kernels: 169 us -> 155 us
    pallas_call x1, Pallas kernels: 169 us -> 155 us  [per_device_gather(): pl.pallas_call(functools.partial(gather_kernel, n_rows), out_shape=(jax.S...]
where the time goes in v3:
time: 162 us; the launch traced here: 161 us
  Pallas kernels  155 us (96%)
  local copies, waits for them, and re-layouts  3.45 us (2%)
  other arithmetic  2.13 us (1%)
    pallas_call x1, Pallas kernels, per_device_gather(): pl.pallas_call(functools.partial(gather_kernel, n_rows), out_shape=(jax.S...  155 us
    unnamed x5, local copies, waits for them, and re-layouts  3.34 us

profile of v3, /device:TPU:0, one launch (start us, length us, event | category | flops | bytes accessed | tf_op | source)
XLA Modules:
  0.0 161.3 jit_solution(9726759951622285868)
XLA Ops:
  0.6 0.0 copy-start
  0.6 0.8 copy.11
  1.4 0.0 copy-done
  1.4 0.1 copy.12
  1.5 1.0 select_reduce_fusion.1.route_in
  2.5 155.0 %shard_map.86 = (bf16[128,2048]{1,0:T(8,128)(2,1)}, bf16[128,128]{1,0:T(8,128)(2,1)}) custom-call(bf16[128,2048]{1,0:T(8,128)(2,1)} %x_in.1, bf16[128,2048]{1,0:T(8,128)(2,1)} %g_in.1, bf16[128,128]{1,0:T(8,128)(2,1)} %select_reduce_fusion.1.route_in, bf16[1024,384]{1,0:T(8,128)(2,1)} %bitcast.3, bf16[1024,384]{1,0:T(8,128)(2,1)} %bitcast.4, ...), custom_call_target="tpu_custom_call" | custom-call | tf_op jit(solution)/shard_map/pallas_call | solution.py:489
  157.6 0.8 convert_element_type.16
  158.3 0.4 select_reduce_fusion
  158.7 0.7 copy.13
  159.4 1.9 %copy.15 = bf16[128,2048]{1,0:T(8,128)(2,1)} copy(bf16[128,2048]{1,0:T(8,128)(2,1)} %get-tuple-element.10) | data formatting | bytes 1048576
Async XLA Ops:
  0.6 0.8 copy-start
